TPU v7x, 128 devices: a whole 4x4x4 slice. The times are simulated.
128 devices in a mesh: site: 4 (over z), blk: 16 (over x, y), charge: 2 (over core).
Axes of the slice: x: 4, y: 4, z: 4, core: 2. Of those that a mesh axis runs over, the one named last changes fastest.
Arguments:
- theta: bfloat16 [4, 64, 128, 2048], P('site', ('blk', 'charge')), may hold values from -6 to 6
- boundary_env: bfloat16 [64, 18, 128, 128], P(('blk', 'charge')), may hold values from -1 to 1
- right_env: bfloat16 [4, 64, 18, 128, 128], P('site', ('blk', 'charge')), may hold values from -1 to 1
- site_tensors: bfloat16 [4, 2, 64, 4, 128, 128], P('site', None, ('blk', 'charge')), may hold values from -0.375 to 0.375
- site_mpo: bfloat16 [4, 2, 18, 18, 4, 4], P('site'), may hold values from -0.75 to 0.75
- bond_ops: bfloat16 [4, 18, 16, 16], P('site'), may hold values from -1 to 1
- block_energy: float32 [4, 64], P('site', ('blk', 'charge')), may hold values from 1 to 4
- sector_charge: int32 [4, 64], P('site', ('blk', 'charge')), may hold values from 0 to 63, as said below
- block_len: int32 [4, 64], P('site', ('blk', 'charge')), may hold values from 64 to 128
- channel_charge: int32 [18], replicated, may hold values from -1 to 1
Outputs:
- env_out: bfloat16 [4, 64, 18, 128, 128], P('site', ('blk', 'charge'))
- lanczos: bfloat16 [4, 64, 128, 2048], P('site', ('blk', 'charge'))
- coefficients: float32 [4, 2], P('site')
Inputs may be any that keep to these rules, and one draw needn't show every extreme that they name: `sector_charge`: in each section every label of 0 to 63 appears exactly once; the blocks held at index c of the charge axis carry labels of parity c.
All inputs are finite; a program needn't handle non-finite values.
Results may differ from a plain program's by a relative error of at most 0.03.
Values may be sent and summed in bfloat16 or wider, within the bound.
A program may use at most 128 MiB of HBM per device.

v0:
```python
import jax
import jax.numpy as jnp
from jax import lax
from jax.sharding import PartitionSpec as P

BS = 128
M = 2048
NS = 64


def from_behind(block, axis, distance):
    devices = range(lax.axis_size(axis))
    route = [(i - distance, i) for i in devices if i - distance in devices]
    return lax.ppermute(block, axis, route)


def from_partner(shard, axis, bit):
    return lax.ppermute(shard, axis, [(i, i ^ 1 << bit) for i in range(lax.axis_size(axis))])


def env_update(environ, tensors, site_op):

    def one_block(entries):
        env_block, site_blocks = entries
        left_part = jnp.einsum(
            "wab,sbc->wsac", env_block, site_blocks, preferred_element_type=jnp.float32
        ).astype(jnp.bfloat16)
        mixed = jnp.einsum(
            "wvts,wsac->vtac", site_op, left_part, preferred_element_type=jnp.float32
        ).astype(jnp.bfloat16)
        return jnp.einsum(
            "tab,vtac->vbc", site_blocks, mixed, preferred_element_type=jnp.float32
        ).astype(jnp.bfloat16)

    return lax.map(one_block, (environ, tensors))


def block_product(env_block, right_blocks, chosen, ops, charges):

    def segment(total_sum, entries):
        left_block, right_block, bond_op, charge = entries
        source_tile = lax.dynamic_index_in_dim(chosen, charge + 1, 0, keepdims=False)
        contracted = jnp.dot(left_block, source_tile, preferred_element_type=jnp.float32).astype(
            jnp.bfloat16
        )
        shaped = contracted.reshape(contracted.shape[0], ops.shape[1], -1)
        applied = jnp.einsum(
            "asb,bc->asc", shaped, right_block, preferred_element_type=jnp.float32
        ).astype(jnp.bfloat16)
        final = jnp.einsum("asc,st->atc", applied, bond_op, preferred_element_type=jnp.float32)
        return (total_sum + final.reshape(total_sum.shape), None)

    start_sum = jnp.zeros((chosen.shape[1], chosen.shape[2]), jnp.float32)
    return lax.scan(segment, start_sum, (env_block, right_blocks, ops, charges))[0]


def keep_same(values):
    return values


def pair_with(environ, tensors, site_ops):
    first = env_update(environ, tensors[0], site_ops[0])
    return env_update(first, tensors[1], site_ops[1])


def picker(wanted_labels, pieces):
    sign_pair = jnp.array([-1, 1], jnp.int32)
    wanted = wanted_labels[:, None] + sign_pair[None, :]
    incoming_tiles, incoming_tags = pieces
    matches = (incoming_tags[None, None, :] == wanted[:, :, None]).astype(jnp.bfloat16)
    picked = jnp.einsum(
        "kst,tam->ksam", matches, incoming_tiles, preferred_element_type=jnp.float32
    )
    return picked.astype(jnp.bfloat16)


def on_device(
    theta,
    boundary_env,
    right_env,
    site_tensors,
    site_mpo,
    bond_ops,
    block_energy,
    sector_charge,
    block_len,
    channel_charge,
):
    section = lax.axis_index("site")
    site_count = lax.axis_size("site")
    tensors = site_tensors[0]
    site_ops = site_mpo[0]

    def update_pair(environ):
        return pair_with(environ, tensors, site_ops)

    state = boundary_env
    env_in = boundary_env
    for segment in range(site_count):
        state = lax.cond(section == segment, update_pair, keep_same, state)
        if segment + 1 < site_count:
            received = from_behind(state, "site", 1)
            is_next = section == segment + 1
            state = jnp.where(is_next, received, state)
            env_in = jnp.where(is_next, received, env_in)
    labels = sector_charge[0]
    live_rows = block_len[0]
    row_mask = jnp.arange(theta.shape[2], dtype=jnp.int32)[None, :] < live_rows[:, None]
    theta_m = theta[0] * row_mask[:, :, None].astype(jnp.bfloat16)
    other_labels = from_partner(labels, "charge", 0)
    for_other = picker(
        other_labels,
        (
            lax.all_gather(theta_m, "blk", axis=0, tiled=True),
            lax.all_gather(labels, "blk", axis=0, tiled=True),
        ),
    )
    partner = from_partner(for_other, "charge", 0)
    chosen_all = jnp.stack([partner[:, 0], theta_m, partner[:, 1]], axis=1)
    ops = bond_ops[0]

    def per_block(entries):
        return block_product(entries[0], entries[1], entries[2], ops, channel_charge)

    product = lax.map(per_block, (env_in, right_env[0], chosen_all))
    theta_f = theta_m.astype(jnp.float32)
    product = (
        product * row_mask[:, :, None].astype(jnp.float32)
        - block_energy[0][:, None, None] * theta_f
    )
    entries_count = NS * BS * M
    correlation, norm_theta = lax.psum(
        (jnp.sum(theta_f * product), jnp.sum(theta_f * theta_f)), ("blk", "charge")
    )
    rayleigh = correlation / norm_theta
    residual = product - rayleigh * theta_f
    residual_sq = lax.psum(jnp.sum(residual * residual), ("blk", "charge"))
    mean_sq = residual_sq / entries_count
    lanczos = (residual / jnp.sqrt(mean_sq + 1e-06)).astype(jnp.bfloat16)
    coefficients = jnp.stack([rayleigh, jnp.sqrt(mean_sq)])[None, :]
    return (state[None], lanczos[None], coefficients)


def solution(mesh):
    return jax.shard_map(
        on_device,
        mesh=mesh,
        in_specs=(
            P("site", ("blk", "charge"), None, None),
            P(("blk", "charge"), None, None, None),
            P("site", ("blk", "charge"), None, None, None),
            P("site", None, ("blk", "charge"), None, None, None),
            P("site", None, None, None, None, None),
            P("site", None, None, None),
            P("site", ("blk", "charge")),
            P("site", ("blk", "charge")),
            P("site", ("blk", "charge")),
            P(),
        ),
        out_specs=(
            P("site", ("blk", "charge"), None, None, None),
            P("site", ("blk", "charge"), None, None),
            P("site", None),
        ),
        check_vma=False,
    )
```

profile of v0, /device:TPU:97, one launch (start us, length us, event | category | flops | bytes accessed | tf_op | source)
XLA Modules:
  0.0 685.1 jit_solution(11959686821084895500)
XLA Ops:
  9.1 2.4 bitcast_multiply_fusion
  18.5 13.5 %all-reduce = s32[32]{0:T(128)S(1)} all-reduce(s32[32]{0:T(128)S(1)} %bitcast_dynamic-update-slice_fusion.1), channel_id=2, replica_groups=mesh['site'=4,'blk'=16,'charge'=2] {'blk'}, use_global_device_ids=true, to_apply=%add | all-reduce | flops 32 | bytes 256
  32.1 11.6 %collective-permute-done = bf16[2,18,128,128]{3,2,1,0:T(8,128)(2,1)S(1)} collective-permute-done((bf16[2,18,128,128]{3,2,1,0:T(8,128)(2,1)}, bf16[2,18,128,128]{3,2,1,0:T(8,128)(2,1)S(1)}, u32[]{:S(2)}, u32[]{:S(2)}) %collective-permute-start) | collective-permute-done | bytes 1179680 | tf_op jit(solution)/shard_map/ppermute | solution.py:14
  43.7 1.8 broadcast_select_fusion
  45.6 1.5 collective-permute-start.1
  47.0 77.2 %all-gather.3.cloned.1.call-done = bf16[32,128,2048]{2,1,0:T(8,128)(2,1)} async-done(((bf16[2,128,2048]{2,1,0:T(8,128)(2,1)}), bf16[32,128,2048]{2,1,0:T(8,128)(2,1)}) %all-gather.3.cloned.1.call-update) | async-done | bytes 16777232 | tf_op jit(solution)/shard_map/all_gather | solution.py:114
  124.2 26.1 %fusion.233 = bf16[2,2,128,2048]{3,1,2,0:T(2,128)(2,1)} fusion(bf16[32,128,2048]{2,1,0:T(8,128)(2,1)} %all-gather.3.cloned.1.call-done, s32[32]{0:T(128)S(1)} %all-reduce, s32[2,2]{1,0:T(2,128)S(1)} %broadcast_add_fusion), kind=kOutput, calls=%fused_computation.203 | convolution fusion | flops 68157568 | bytes 18874512 | tf_op jit(solution)/shard_map/kst,tam->ksam/dot_general | solution.py:71
  151.6 9.2 %collective-permute-start.2 = (bf16[2,18,128,128]{3,2,1,0:T(8,128)(2,1)S(1)}, bf16[2,18,128,128]{3,2,1,0:T(8,128)(2,1)}, u32[]{:S(2)}, u32[]{:S(2)}) collective-permute-start(bf16[2,18,128,128]{3,2,1,0:T(8,128)(2,1)S(1)} %get-tuple-element.589), channel_id=1, source_target_pairs={{0,32},{32,64},{64,96},{1,33},{33,65},{65,97},{2,34},{34,66},{66,9... | collective-permute-start | bytes 3538952 | tf_op jit(solution)/shard_map/ppermute | solution.py:14
  160.8 1.7 copy.99
  162.5 2.2 copy_multiply_fusion
  164.7 85.6 %collective-permute-done.2 = bf16[2,18,128,128]{3,2,1,0:T(8,128)(2,1)} collective-permute-done((bf16[2,18,128,128]{3,2,1,0:T(8,128)(2,1)S(1)}, bf16[2,18,128,128]{3,2,1,0:T(8,128)(2,1)}, u32[]{:S(2)}, u32[]{:S(2)}) %collective-permute-start.2) | collective-permute-done | bytes 1179680 | tf_op jit(solution)/shard_map/ppermute | solution.py:14
  250.4 2.7 select_select_fusion
  253.1 5.6 fusion.247
  258.6 7.1 %pad_maximum_fusion = bf16[2,3,128,2048]{3,1,2,0:T(4,128)(2,1)S(1)} fusion(bf16[2,1,128,2048]{3,1,2,0:T(2,128)(2,1)S(1)} %get-tuple-element.724, bf16[2,1,128,2048]{3,1,2,0:T(2,128)(2,1)S(1)} %copy_multiply_fusion, bf16[2,1,128,2048]{3,1,2,0:T(2,128)(2,1)S(1)} %get-tuple-element.723), kind=kLoop, calls=%fused_computation.198 | loop fusion | flops 9437184 | bytes 6291456 | tf_op jit(solution)/shard_map/stack | solution.py:119
  265.8 3.9 copy.100
  269.7 211.9 %while.113 = (s32[]{:T(128)}, f32[2,128,2048]{2,1,0:T(8,128)}, bf16[2,18,128,128]{3,2,1,0:T(8,128)(2,1)S(1)}, bf16[2,18,128,128]{3,2,1,0:T(8,128)(2,1)}, bf16[2,...) while((s32[]{:T(128)}, f32[2,128,2048]{2,1,0:T(8,128)}, ...), condition=%wide.region_27.28_spmd, body=%wide.region_24.27_spmd.sunk | while | flops 143654912 | bytes 23926256 | solution.py:125
  269.7 2.4 dynamic-slice_bitcast_fusion.5
  272.1 2.7 dynamic-slice_bitcast_fusion.6
  274.8 99.1 %while.114 = (s32[]{:T(128)}, f32[128,2048]{1,0:T(8,128)S(1)}, bf16[18,16,16]{1,2,0:T(8,128)(2,1)}, bf16[18,128,128]{2,1,0:T(8,128)(2,1)}, s32[18]{0:T(128)S(1)}...) while((s32[]{:T(128)}, f32[128,2048]{1,0:T(8,128)S(1)}, ...), condition=%wide.region_26.26_spmd.clone, body=%wide.region_25.25_spmd.clone.sunk | while | flops 143654912 | bytes 6886593 | solution.py:54
  375.6 2.4 dynamic-slice_bitcast_fusion.5
  378.0 2.7 dynamic-slice_bitcast_fusion.6
  380.7 99.1 %while.114 = (s32[]{:T(128)}, f32[128,2048]{1,0:T(8,128)S(1)}, bf16[18,16,16]{1,2,0:T(8,128)(2,1)}, bf16[18,128,128]{2,1,0:T(8,128)(2,1)}, s32[18]{0:T(128)S(1)}...) while((s32[]{:T(128)}, f32[128,2048]{1,0:T(8,128)S(1)}, ...), condition=%wide.region_26.26_spmd.clone, body=%wide.region_25.25_spmd.clone.sunk | while | flops 143654912 | bytes 6886593 | solution.py:54
  382.8 1.4 fusion.325
  399.3 1.4 fusion.325
  415.8 1.4 fusion.325
  481.5 3.8 fusion.238
  485.3 68.7 %all-reduce.1 = (f32[]{:T(128)}, f32[]{:T(128)}) all-reduce(f32[]{:T(128)} %get-tuple-element.594, f32[]{:T(128)} %get-tuple-element.593), channel_id=1, replica_groups=mesh['site'=4,'blk'=16,'charge'=2] {'blk','charge'}, use_global_device_ids=true, to_apply=%region_29.30 | all-reduce | flops 2 | bytes 16 | tf_op jit(solution)/shard_map/psum | solution.py:132
  555.4 3.3 multiply_reduce_fusion
  558.7 48.6 %conditional.7 = (bf16[1,2,18,128,128]{4,3,2,1,0:T(8,128)(2,1)}) conditional(s32[]{:T(128)} %convert_element_type.194, (bf16[2,18,128,128]{3,2,1,0:T(8,128)(2,1)S(1)}) %tuple.289, (bf16[2,2,4,128,128]{3,4,2,1,0:T(8,128)(2,1)}, bf16[2,18,18,4,4]{1,2,4,3,0:T(8,128)(2,1)}, bf16[2,18,128,128]{3,2,1,0:T(8,128)(2,1)S(1)}) %tuple.290), branch_computations={%region_18.19_spmd, %region_19.24_spmd} | conditional | flops 1553006592 | bytes 31303274 | solution.py:100
  558.7 1.9 slice_bitcast_fusion.12
  560.6 1.6 slice_bitcast_fusion.14
  562.5 21.7 %while.109 = (s32[]{:T(128)}, bf16[2,18,128,128]{2,3,1,0:T(8,128)(2,1)S(1)}, bf16[2,4,128,128]{2,3,1,0:T(8,128)(2,1)}, bf16[2,18,128,128]{3,2,1,0:T(8,128)(2,1)S(1)}, bf16[18,18,4,4]{0,1,3,2:T(8,128)(2,1)}, /*index=5*/s32[]{:T(128)}) while((s32[]{:T(128)}, bf16[2,18,128,128]{2,3,1,0:T(8,128)(2,1)S(1)}, bf16[2,4,128,128]{2,3,1,0:T(8,128)(2,1)}, ...), condition=%wide.region_21.21_spmd, body=%wide.region_20.20_spmd.sunk | while | flops 776503296 | bytes 12768005 | solution.py:35
  562.7 1.7 convert_bitcast_fusion.16
  564.4 7.2 %fusion.333 = bf16[18,4,128,128]{2,0,1,3:T(8,128)(2,1)S(1)} fusion(bf16[18,4,128,128,1]{2,3,0,1,4:T(8,128)(2,1)S(1)} %convert_bitcast_fusion.16, bf16[18,18,4,4]{0,1,3,2:T(8,128)(2,1)S(1)} %copy-done.20), kind=kOutput, calls=%fused_computation.133.clone.1 | convolution fusion | flops 171048960 | bytes 4728960 | tf_op jit(solution)/shard_map/cond/branch_1_fun/while/body/eval_jaxpr/wvts,wsac->vtac/dot_general | solution.py:28
  571.6 1.7 fusion.334
  573.4 1.7 convert_bitcast_fusion.16
  575.2 7.2 %fusion.333 = bf16[18,4,128,128]{2,0,1,3:T(8,128)(2,1)S(1)} fusion(bf16[18,4,128,128,1]{2,3,0,1,4:T(8,128)(2,1)S(1)} %convert_bitcast_fusion.16, bf16[18,18,4,4]{0,1,3,2:T(8,128)(2,1)S(1)} %copy-done.20), kind=kOutput, calls=%fused_computation.133.clone.1 | convolution fusion | flops 171048960 | bytes 4728960 | tf_op jit(solution)/shard_map/cond/branch_1_fun/while/body/eval_jaxpr/wvts,wsac->vtac/dot_general | solution.py:28
  582.4 1.7 fusion.334
  584.4 21.3 %while.110 = (s32[]{:T(128)}, bf16[2,18,128,128]{2,3,1,0:T(8,128)(2,1)S(1)}, bf16[2,4,128,128]{2,3,1,0:T(8,128)(2,1)}, bf16[2,18,128,128]{2,3,1,0:T(8,128)(2,1)S...) while((s32[]{:T(128)}, bf16[2,18,128,128]{2,3,1,0:T(8,128)(2,1)S(1)}, ...), condition=%wide.region_23.23_spmd, body=%wide.region_22.22_spmd.sunk | while | flops 776503296 | bytes 12726505 | solution.py:35
  584.4 1.7 convert_bitcast_fusion.17
  586.1 7.2 %fusion.341 = bf16[18,4,128,128]{2,0,1,3:T(8,128)(2,1)S(1)} fusion(bf16[18,4,128,128,1]{2,3,0,1,4:T(8,128)(2,1)S(1)} %convert_bitcast_fusion.17, bf16[18,18,4,4]{0,1,3,2:T(8,128)(2,1)S(1)} %get-tuple-element.1151), kind=kOutput, calls=%fused_computation.153.clone.1 | convolution fusion | flops 171048960 | bytes 4728960 | tf_op jit(solution)/shard_map/cond/branch_1_fun/while/body/eval_jaxpr/wvts,wsac->vtac/dot_general | solution.py:28
  593.3 1.7 fusion.342
  595.1 1.7 convert_bitcast_fusion.17
  596.8 7.2 %fusion.341 = bf16[18,4,128,128]{2,0,1,3:T(8,128)(2,1)S(1)} fusion(bf16[18,4,128,128,1]{2,3,0,1,4:T(8,128)(2,1)S(1)} %convert_bitcast_fusion.17, bf16[18,18,4,4]{0,1,3,2:T(8,128)(2,1)S(1)} %get-tuple-element.1151), kind=kOutput, calls=%fused_computation.153.clone.1 | convolution fusion | flops 171048960 | bytes 4728960 | tf_op jit(solution)/shard_map/cond/branch_1_fun/while/body/eval_jaxpr/wvts,wsac->vtac/dot_general | solution.py:28
  604.0 1.7 fusion.342
  605.7 1.4 copy.177
  607.4 65.9 %psum.23 = f32[]{:T(128)} all-reduce(f32[]{:T(128)} %multiply_reduce_fusion), channel_id=1, replica_groups=mesh['site'=4,'blk'=16,'charge'=2] {'blk','charge'}, use_global_device_ids=true, to_apply=%region_33.34 | all-reduce | flops 1 | bytes 8 | tf_op jit(solution)/shard_map/psum | solution.py:137
  674.0 3.3 fusion.240
  (257 shorter events, 158.0 us)
Async XLA Ops:
  7.2 4.4 copy-start.18
  7.2 5.4 copy-start.17
  7.2 117.0 %all-gather.3.cloned.1.call-start = ((), (), s32[]{:S(2)}) async-start(), calls=%async_computation | async-start | bytes 17825792 | tf_op jit(solution)/shard_map/all_gather | solution.py:114
  8.6 0.5 copy-start.21
  9.1 4.5 copy-start.2
  13.6 2.3 copy-start.26
  13.6 3.4 copy-start.28
  13.6 18.4 %copy-start.25 = (s32[2]{0:T(128)S(1)}, s32[2]{0:T(128)}, u32[]{:S(2)}) copy-start(s32[2]{0:T(128)} %constant.168.clone) | copy-start | bytes 28
  14.7 29.0 %collective-permute-start = (bf16[2,18,128,128]{3,2,1,0:T(8,128)(2,1)}, bf16[2,18,128,128]{3,2,1,0:T(8,128)(2,1)S(1)}, u32[]{:S(2)}, u32[]{:S(2)}) collective-permute-start(bf16[2,18,128,128]{3,2,1,0:T(8,128)(2,1)} %get-tuple-element.585), channel_id=1, source_target_pairs={{0,32},{32,64},{64,96},{1,33},{33,65},{65,97},{2,34},{34,66},{66,9... | collective-permute-start | bytes 3538952 | tf_op jit(solution)/shard_map/ppermute | solution.py:14
  16.0 16.0 %collective-permute-start.3 = (s32[2]{0:T(128)S(1)}, s32[2]{0:T(128)S(1)}, u32[]{:S(2)}, u32[]{:S(2)}) collective-permute-start(s32[2]{0:T(128)S(1)} %bitcast.620), channel_id=1, source_target_pairs={{0,1},{1,0},{2,3},{3,2},{4,5},{5,4},{6,7},{7,6},{8,9},{9,8},{10,11... | collective-permute-start | bytes 32 | tf_op jit(solution)/shard_map/ppermute | solution.py:18
  43.7 1.8 copy-start.8
  45.6 105.5 %collective-permute-start.1 = (bf16[2,18,128,128]{3,2,1,0:T(8,128)(2,1)S(1)}, bf16[2,18,128,128]{3,2,1,0:T(8,128)(2,1)}, u32[]{:S(2)}, u32[]{:S(2)}) collective-permute-start(bf16[2,18,128,128]{3,2,1,0:T(8,128)(2,1)S(1)} %get-tuple-element.587), channel_id=1, source_target_pairs={{0,32},{32,64},{64,96},{1,33},{33,65},{65,97},{2,34},{34,66},{66,9... | collective-permute-start | bytes 3538952 | tf_op jit(solution)/shard_map/ppermute | solution.py:14
  150.3 102.7 %collective-permute-start.4 = (bf16[2,2,128,2048]{3,1,2,0:T(2,128)(2,1)}, bf16[2,2,128,2048]{3,1,2,0:T(2,128)(2,1)}, u32[]{:S(2)}, u32[]{:S(2)}) collective-permute-start(bf16[2,2,128,2048]{3,1,2,0:T(2,128)(2,1)} %fusion.233), channel_id=1, source_target_pairs={{0,1},{1,0},{2,3},{3,2},{4,5},{5,4},{6,7},{7,6},{8,9},{9,8},{10,11... | collective-permute-start | bytes 6291464 | tf_op jit(solution)/shard_map/ppermute | solution.py:18
  151.2 11.3 %copy-start = (bf16[1,2,128,2048]{3,2,1,0:T(8,128)(2,1)S(1)}, bf16[1,2,128,2048]{3,2,1,0:T(8,128)(2,1)}, u32[]{:S(2)}) copy-start(bf16[1,2,128,2048]{3,2,1,0:T(8,128)(2,1)} %param.39) | copy-start | bytes 3145732
  151.2 11.3 %copy-start.22 = (bf16[2,128]{1,0:T(2,128)(2,1)S(1)}, bf16[2,128]{1,0:T(2,128)(2,1)}, u32[]{:S(2)}) copy-start(bf16[2,128]{1,0:T(2,128)(2,1)} %copy-done.21) | copy-start | bytes 1540
  151.6 98.7 %collective-permute-start.2 = (bf16[2,18,128,128]{3,2,1,0:T(8,128)(2,1)S(1)}, bf16[2,18,128,128]{3,2,1,0:T(8,128)(2,1)}, u32[]{:S(2)}, u32[]{:S(2)}) collective-permute-start(bf16[2,18,128,128]{3,2,1,0:T(8,128)(2,1)S(1)} %get-tuple-element.589), channel_id=1, source_target_pairs={{0,32},{32,64},{64,96},{1,33},{33,65},{65,97},{2,34},{34,66},{66,9... | collective-permute-start | bytes 3538952 | tf_op jit(solution)/shard_map/ppermute | solution.py:14
  162.5 87.9 %copy-start.9 = (bf16[2,18,128,128]{3,2,1,0:T(8,128)(2,1)S(1)}, bf16[2,18,128,128]{3,2,1,0:T(8,128)(2,1)}, u32[]{:S(2)}) copy-start(bf16[2,18,128,128]{3,2,1,0:T(8,128)(2,1)} %copy-done.8) | copy-start | bytes 3538948
  265.8 3.9 copy-start.27
  269.7 211.9 %copy-start.23 = (f32[2,128]{1,0:T(2,128)S(1)}, f32[2,128]{1,0:T(2,128)}, u32[]{:S(2)}) copy-start(f32[2,128]{1,0:T(2,128)} %get-tuple-element.727) | copy-start | bytes 3076
  269.7 211.9 %copy-start.24 = (f32[1,2]{1,0:T(1,128)S(1)}, f32[1,2]{1,0:T(1,128)}, u32[]{:S(2)}) copy-start(f32[1,2]{1,0:T(1,128)} %param.45) | copy-start | bytes 28
  269.7 5.2 copy-start.4
  374.0 1.6 copy-start.5
  375.6 5.1 copy-start.4
  479.9 1.6 copy-start.5
  481.5 73.8 %copy-start.1 = (bf16[1,2,128,2048]{3,2,1,0:T(8,128)(2,1)S(1)}, bf16[1,2,128,2048]{3,2,1,0:T(8,128)(2,1)}, u32[]{:S(2)}) copy-start(bf16[1,2,128,2048]{3,2,1,0:T(8,128)(2,1)} %param.39) | copy-start | bytes 3145732
  481.5 73.8 %copy-start.3 = (bf16[2,18,128,128]{3,2,1,0:T(8,128)(2,1)S(1)}, bf16[2,18,128,128]{3,2,1,0:T(8,128)(2,1)}, u32[]{:S(2)}) copy-start(bf16[2,18,128,128]{3,2,1,0:T(8,128)(2,1)} %get-tuple-element.726) | copy-start | bytes 3538948
  562.7 1.7 copy-start.20
  564.4 7.2 %copy-start.14 = (bf16[2,4,128,128]{2,3,1,0:T(8,128)(2,1)S(1)}, bf16[2,4,128,128]{2,3,1,0:T(8,128)(2,1)}, u32[]{:S(2)}) copy-start(bf16[2,4,128,128]{2,3,1,0:T(8,128)(2,1)} %get-tuple-element.1131) | copy-start | bytes 786436 | tf_op jit(solution)/shard_map/cond/branch_1_fun/while
  573.4 1.7 copy-start.20
  575.2 7.2 %copy-start.14 = (bf16[2,4,128,128]{2,3,1,0:T(8,128)(2,1)S(1)}, bf16[2,4,128,128]{2,3,1,0:T(8,128)(2,1)}, u32[]{:S(2)}) copy-start(bf16[2,4,128,128]{2,3,1,0:T(8,128)(2,1)} %get-tuple-element.1131) | copy-start | bytes 786436 | tf_op jit(solution)/shard_map/cond/branch_1_fun/while
  586.1 7.2 %copy-start.11 = (bf16[2,4,128,128]{2,3,1,0:T(8,128)(2,1)S(1)}, bf16[2,4,128,128]{2,3,1,0:T(8,128)(2,1)}, u32[]{:S(2)}) copy-start(bf16[2,4,128,128]{2,3,1,0:T(8,128)(2,1)} %get-tuple-element.1149) | copy-start | bytes 786436 | tf_op jit(solution)/shard_map/cond/branch_1_fun/while
  596.7 7.2 %copy-start.11 = (bf16[2,4,128,128]{2,3,1,0:T(8,128)(2,1)S(1)}, bf16[2,4,128,128]{2,3,1,0:T(8,128)(2,1)}, u32[]{:S(2)}) copy-start(bf16[2,4,128,128]{2,3,1,0:T(8,128)(2,1)} %get-tuple-element.1149) | copy-start | bytes 786436 | tf_op jit(solution)/shard_map/cond/branch_1_fun/while
Sparse Core Ops, SparseCore 0:
  11.7 112.4 all-gather.2
where the time goes:
time: 698 us; the launch traced here: 685 us
  waiting for transfers between devices  174 us (25%)
  matrix products  161 us (23%)
  blocking collectives  148 us (21%)
  local copies, waits for them, and re-layouts  62.4 us (9%)
  other arithmetic  56 us (8%)
  loops' own time  52.4 us (8%)
  between operations  17.4 us (2%)
  starting transfers between devices  13.8 us (2%)
    ppermute x3, waiting for transfers between devices, from_behind(): return lax.ppermute(block, axis, route)  97.3 us
    all_gather x1, waiting for transfers between devices, on_device(): lax.all_gather(theta_m, 'blk', axis=0, tiled=True)  77.2 us
    psum x1, blocking collectives, on_device(): lax.psum((jnp.sum(theta_f * product), jnp.sum(theta_f * theta_f)), ('blk'...  68.7 us
    psum x1, blocking collectives, on_device(): residual_sq = lax.psum(jnp.sum(residual * residual), ('blk', 'charge'))  65.9 us
    another operation x2, loops' own time, block_product(): lax.scan(segment, start_sum, (env_block, right_blocks, ops, charges))[0]  51.2 us
    dot_general x36, matrix products, segment(): jnp.dot(left_block, source_tile, preferred_element_type=jnp.float32)  48.7 us
    dot_general x36, matrix products, segment(): jnp.einsum('asc,st->atc', applied, bond_op, preferred_element_type=jnp.fl...  43.4 us
    dot_general x4, matrix products, one_block(): jnp.einsum('wvts,wsac->vtac', site_op, left_part, preferred_element_type=...  28.8 us
  transfers between devices with their start and end apart: 6, of which 3 were waited for; matrix products, arithmetic and copies ran while one was open for 6% of the time, Pallas kernels for 0%

commit v1 on v0

--- a/solution.py
+++ b/solution.py
@@ -130,7 +130,7 @@
     )
     entries_count = NS * BS * M
     correlation, norm_theta = lax.psum(
-        (jnp.sum(theta_f * product), jnp.sum(theta_f * theta_f)), ("blk", "charge")
+        lax.psum((jnp.sum(theta_f * product), jnp.sum(theta_f * theta_f)), "blk"), "charge"
     )
     rayleigh = correlation / norm_theta
     residual = product - rayleigh * theta_f

time: 698 us -> 664 us (0.951)
  blocking collectives: 148 us -> 126 us
  loops' own time: 52.4 us -> 43.2 us
    psum x1 -> x2, blocking collectives: 68.7 us -> 49.8 us  [the longest x1 37.4 us: on_device(): lax.psum((jnp.sum(theta_f * product), jnp.sum(theta_f * theta_f)), 'blk')]
    another operation x2, loops' own time: 51.2 us -> 42 us  [block_product(): lax.scan(segment, start_sum, (env_block, right_blocks, ops, charges))[0]]
where the time goes in v1:
time: 664 us; the launch traced here: 651 us
  waiting for transfers between devices  174 us (26%)
  matrix products  161 us (24%)
  blocking collectives  126 us (19%)
  local copies, waits for them, and re-layouts  59.4 us (9%)
  other arithmetic  55.9 us (8%)
  loops' own time  43.2 us (7%)
  between operations  17.5 us (3%)
  starting transfers between devices  13.8 us (2%)
    ppermute x3, waiting for transfers between devices, from_behind(): return lax.ppermute(block, axis, route)  97.2 us
    all_gather x1, waiting for transfers between devices, on_device(): lax.all_gather(theta_m, 'blk', axis=0, tiled=True)  77.2 us
    psum x1, blocking collectives, on_device(): residual_sq = lax.psum(jnp.sum(residual * residual), ('blk', 'charge'))  62.9 us
    dot_general x36, matrix products, segment(): jnp.dot(left_block, source_tile, preferred_element_type=jnp.float32)  48.7 us
    dot_general x36, matrix products, segment(): jnp.einsum('asc,st->atc', applied, bond_op, preferred_element_type=jnp.fl...  43.4 us
    another operation x2, loops' own time, block_product(): lax.scan(segment, start_sum, (env_block, right_blocks, ops, charges))[0]  42 us
    psum x1, blocking collectives, on_device(): lax.psum((jnp.sum(theta_f * product), jnp.sum(theta_f * theta_f)), 'blk')  37.4 us
    dot_general x4, matrix products, one_block(): jnp.einsum('wvts,wsac->vtac', site_op, left_part, preferred_element_type=...  28.8 us
  transfers between devices with their start and end apart: 6, of which 3 were waited for; matrix products, arithmetic and copies ran while one was open for 6% of the time, Pallas kernels for 0%

profile of v1, /device:TPU:97, one launch (start us, length us, event | category | flops | bytes accessed | tf_op | source)
XLA Modules:
  0.0 651.1 jit_solution(7070397695533457432)
XLA Ops:
  7.2 1.4 fusion.244
  9.1 2.4 bitcast_multiply_fusion
  18.5 13.5 %all-reduce = s32[32]{0:T(128)S(1)} all-reduce(s32[32]{0:T(128)S(1)} %bitcast_dynamic-update-slice_fusion.1), channel_id=2, replica_groups=mesh['site'=4,'blk'=16,'charge'=2] {'blk'}, use_global_device_ids=true, to_apply=%add | all-reduce | flops 32 | bytes 256
  32.1 11.6 %collective-permute-done = bf16[2,18,128,128]{3,2,1,0:T(8,128)(2,1)S(1)} collective-permute-done((bf16[2,18,128,128]{3,2,1,0:T(8,128)(2,1)}, bf16[2,18,128,128]{3,2,1,0:T(8,128)(2,1)S(1)}, u32[]{:S(2)}, u32[]{:S(2)}) %collective-permute-start) | collective-permute-done | bytes 1179680 | tf_op jit(solution)/shard_map/ppermute | solution.py:14
  43.7 1.8 broadcast_select_fusion
  45.6 1.5 collective-permute-start.1
  47.0 77.2 %all-gather.3.cloned.1.call-done = bf16[32,128,2048]{2,1,0:T(8,128)(2,1)} async-done(((bf16[2,128,2048]{2,1,0:T(8,128)(2,1)}), bf16[32,128,2048]{2,1,0:T(8,128)(2,1)}) %all-gather.3.cloned.1.call-update) | async-done | bytes 16777232 | tf_op jit(solution)/shard_map/all_gather | solution.py:114
  124.2 26.1 %fusion.233 = bf16[2,2,128,2048]{3,1,2,0:T(2,128)(2,1)} fusion(bf16[32,128,2048]{2,1,0:T(8,128)(2,1)} %all-gather.3.cloned.1.call-done, s32[32]{0:T(128)S(1)} %all-reduce, s32[2,2]{1,0:T(2,128)S(1)} %broadcast_add_fusion), kind=kOutput, calls=%fused_computation.203 | convolution fusion | flops 68157568 | bytes 18874512 | tf_op jit(solution)/shard_map/kst,tam->ksam/dot_general | solution.py:71
  151.6 9.2 %collective-permute-start.2 = (bf16[2,18,128,128]{3,2,1,0:T(8,128)(2,1)S(1)}, bf16[2,18,128,128]{3,2,1,0:T(8,128)(2,1)}, u32[]{:S(2)}, u32[]{:S(2)}) collective-permute-start(bf16[2,18,128,128]{3,2,1,0:T(8,128)(2,1)S(1)} %get-tuple-element.589), channel_id=1, source_target_pairs={{0,32},{32,64},{64,96},{1,33},{33,65},{65,97},{2,34},{34,66},{66,9... | collective-permute-start | bytes 3538952 | tf_op jit(solution)/shard_map/ppermute | solution.py:14
  160.9 1.7 copy.99
  162.5 2.2 copy_multiply_fusion
  164.8 85.6 %collective-permute-done.2 = bf16[2,18,128,128]{3,2,1,0:T(8,128)(2,1)} collective-permute-done((bf16[2,18,128,128]{3,2,1,0:T(8,128)(2,1)S(1)}, bf16[2,18,128,128]{3,2,1,0:T(8,128)(2,1)}, u32[]{:S(2)}, u32[]{:S(2)}) %collective-permute-start.2) | collective-permute-done | bytes 1179680 | tf_op jit(solution)/shard_map/ppermute | solution.py:14
  250.4 2.7 select_select_fusion
  253.1 5.6 fusion.247
  258.7 7.1 %pad_maximum_fusion = bf16[2,3,128,2048]{3,1,2,0:T(4,128)(2,1)S(1)} fusion(bf16[2,1,128,2048]{3,1,2,0:T(2,128)(2,1)S(1)} %get-tuple-element.726, bf16[2,1,128,2048]{3,1,2,0:T(2,128)(2,1)S(1)} %copy_multiply_fusion, bf16[2,1,128,2048]{3,1,2,0:T(2,128)(2,1)S(1)} %get-tuple-element.725), kind=kLoop, calls=%fused_computation.198 | loop fusion | flops 9437184 | bytes 6291456 | tf_op jit(solution)/shard_map/stack | solution.py:119
  265.8 3.9 copy.100
  269.7 199.8 %while.113 = (s32[]{:T(128)}, f32[2,128,2048]{2,1,0:T(8,128)}, bf16[2,18,128,128]{3,2,1,0:T(8,128)(2,1)S(1)}, bf16[2,18,128,128]{3,2,1,0:T(8,128)(2,1)}, bf16[2,...) while((s32[]{:T(128)}, f32[2,128,2048]{2,1,0:T(8,128)}, ...), condition=%wide.region_27.28_spmd, body=%wide.region_24.27_spmd.sunk | while | flops 143654912 | bytes 23926256 | solution.py:125
  269.7 2.4 dynamic-slice_bitcast_fusion.5
  272.1 2.8 dynamic-slice_bitcast_fusion.6
  274.9 93.1 %while.114 = (s32[]{:T(128)}, f32[128,2048]{1,0:T(8,128)S(1)}, bf16[18,16,16]{1,2,0:T(8,128)(2,1)}, bf16[18,128,128]{2,1,0:T(8,128)(2,1)}, s32[18]{0:T(128)S(1)}...) while((s32[]{:T(128)}, f32[128,2048]{1,0:T(8,128)S(1)}, ...), condition=%wide.region_26.26_spmd.clone, body=%wide.region_25.25_spmd.clone.sunk | while | flops 143654912 | bytes 6886593 | solution.py:54
  307.6 1.4 fusion.325
  369.6 2.4 dynamic-slice_bitcast_fusion.5
  372.0 2.8 dynamic-slice_bitcast_fusion.6
  374.8 93.1 %while.114 = (s32[]{:T(128)}, f32[128,2048]{1,0:T(8,128)S(1)}, bf16[18,16,16]{1,2,0:T(8,128)(2,1)}, bf16[18,128,128]{2,1,0:T(8,128)(2,1)}, s32[18]{0:T(128)S(1)}...) while((s32[]{:T(128)}, f32[128,2048]{1,0:T(8,128)S(1)}, ...), condition=%wide.region_26.26_spmd.clone, body=%wide.region_25.25_spmd.clone.sunk | while | flops 143654912 | bytes 6886593 | solution.py:54
  469.5 3.8 fusion.238
  473.3 37.4 %all-reduce.1 = (f32[]{:T(128)}, f32[]{:T(128)}) all-reduce(f32[]{:T(128)} %get-tuple-element.594, f32[]{:T(128)} %get-tuple-element.593), channel_id=1, replica_groups=mesh['site'=4,'blk'=16,'charge'=2] {'blk'}, use_global_device_ids=true, to_apply=%region_29.30 | all-reduce | flops 2 | bytes 16 | tf_op jit(solution)/shard_map/psum | solution.py:133
  510.7 12.4 %all-reduce.2 = (f32[]{:T(128)}, f32[]{:T(128)}) all-reduce(f32[]{:T(128)} %get-tuple-element.703, f32[]{:T(128)} %get-tuple-element.704), channel_id=1, replica_groups=mesh['site'=4,'blk'=16,'charge'=2] {'charge'}, use_global_device_ids=true, to_apply=%region_30.31 | all-reduce | flops 2 | bytes 16 | tf_op jit(solution)/shard_map/psum | solution.py:132
  524.5 3.2 multiply_reduce_fusion
  527.7 48.6 %conditional.7 = (bf16[1,2,18,128,128]{4,3,2,1,0:T(8,128)(2,1)}) conditional(s32[]{:T(128)} %convert_element_type.194, (bf16[2,18,128,128]{3,2,1,0:T(8,128)(2,1)S(1)}) %tuple.289, (bf16[2,2,4,128,128]{3,4,2,1,0:T(8,128)(2,1)}, bf16[2,18,18,4,4]{1,2,4,3,0:T(8,128)(2,1)}, bf16[2,18,128,128]{3,2,1,0:T(8,128)(2,1)S(1)}) %tuple.290), branch_computations={%region_18.19_spmd, %region_19.24_spmd} | conditional | flops 1553006592 | bytes 31303274 | solution.py:100
  527.7 1.9 slice_bitcast_fusion.12
  529.6 1.6 slice_bitcast_fusion.14
  531.5 21.7 %while.109 = (s32[]{:T(128)}, bf16[2,18,128,128]{2,3,1,0:T(8,128)(2,1)S(1)}, bf16[2,4,128,128]{2,3,1,0:T(8,128)(2,1)}, bf16[2,18,128,128]{3,2,1,0:T(8,128)(2,1)S(1)}, bf16[18,18,4,4]{0,1,3,2:T(8,128)(2,1)}, /*index=5*/s32[]{:T(128)}) while((s32[]{:T(128)}, bf16[2,18,128,128]{2,3,1,0:T(8,128)(2,1)S(1)}, bf16[2,4,128,128]{2,3,1,0:T(8,128)(2,1)}, ...), condition=%wide.region_21.21_spmd, body=%wide.region_20.20_spmd.sunk | while | flops 776503296 | bytes 12768005 | solution.py:35
  531.7 1.7 convert_bitcast_fusion.16
  533.5 7.2 %fusion.333 = bf16[18,4,128,128]{2,0,1,3:T(8,128)(2,1)S(1)} fusion(bf16[18,4,128,128,1]{2,3,0,1,4:T(8,128)(2,1)S(1)} %convert_bitcast_fusion.16, bf16[18,18,4,4]{0,1,3,2:T(8,128)(2,1)S(1)} %copy-done.20), kind=kOutput, calls=%fused_computation.133.clone.1 | convolution fusion | flops 171048960 | bytes 4728960 | tf_op jit(solution)/shard_map/cond/branch_1_fun/while/body/eval_jaxpr/wvts,wsac->vtac/dot_general | solution.py:28
  540.7 1.7 fusion.334
  542.4 1.7 convert_bitcast_fusion.16
  544.2 7.2 %fusion.333 = bf16[18,4,128,128]{2,0,1,3:T(8,128)(2,1)S(1)} fusion(bf16[18,4,128,128,1]{2,3,0,1,4:T(8,128)(2,1)S(1)} %convert_bitcast_fusion.16, bf16[18,18,4,4]{0,1,3,2:T(8,128)(2,1)S(1)} %copy-done.20), kind=kOutput, calls=%fused_computation.133.clone.1 | convolution fusion | flops 171048960 | bytes 4728960 | tf_op jit(solution)/shard_map/cond/branch_1_fun/while/body/eval_jaxpr/wvts,wsac->vtac/dot_general | solution.py:28
  551.4 1.7 fusion.334
  553.4 21.3 %while.110 = (s32[]{:T(128)}, bf16[2,18,128,128]{2,3,1,0:T(8,128)(2,1)S(1)}, bf16[2,4,128,128]{2,3,1,0:T(8,128)(2,1)}, bf16[2,18,128,128]{2,3,1,0:T(8,128)(2,1)S...) while((s32[]{:T(128)}, bf16[2,18,128,128]{2,3,1,0:T(8,128)(2,1)S(1)}, ...), condition=%wide.region_23.23_spmd, body=%wide.region_22.22_spmd.sunk | while | flops 776503296 | bytes 12726505 | solution.py:35
  553.4 1.7 convert_bitcast_fusion.17
  555.1 7.2 %fusion.341 = bf16[18,4,128,128]{2,0,1,3:T(8,128)(2,1)S(1)} fusion(bf16[18,4,128,128,1]{2,3,0,1,4:T(8,128)(2,1)S(1)} %convert_bitcast_fusion.17, bf16[18,18,4,4]{0,1,3,2:T(8,128)(2,1)S(1)} %get-tuple-element.1153), kind=kOutput, calls=%fused_computation.153.clone.1 | convolution fusion | flops 171048960 | bytes 4728960 | tf_op jit(solution)/shard_map/cond/branch_1_fun/while/body/eval_jaxpr/wvts,wsac->vtac/dot_general | solution.py:28
  562.3 1.7 fusion.342
  564.1 1.7 convert_bitcast_fusion.17
  565.8 7.2 %fusion.341 = bf16[18,4,128,128]{2,0,1,3:T(8,128)(2,1)S(1)} fusion(bf16[18,4,128,128,1]{2,3,0,1,4:T(8,128)(2,1)S(1)} %convert_bitcast_fusion.17, bf16[18,18,4,4]{0,1,3,2:T(8,128)(2,1)S(1)} %get-tuple-element.1153), kind=kOutput, calls=%fused_computation.153.clone.1 | convolution fusion | flops 171048960 | bytes 4728960 | tf_op jit(solution)/shard_map/cond/branch_1_fun/while/body/eval_jaxpr/wvts,wsac->vtac/dot_general | solution.py:28
  573.0 1.7 fusion.342
  574.7 1.4 copy.177
  576.4 62.9 %psum.39 = f32[]{:T(128)} all-reduce(f32[]{:T(128)} %multiply_reduce_fusion), channel_id=1, replica_groups=mesh['site'=4,'blk'=16,'charge'=2] {'blk','charge'}, use_global_device_ids=true, to_apply=%region_35.36 | all-reduce | flops 1 | bytes 8 | tf_op jit(solution)/shard_map/psum | solution.py:137
  640.0 3.3 fusion.240
  (258 shorter events, 156.4 us)
Async XLA Ops:
  7.2 4.4 copy-start.18
  7.2 5.4 copy-start.17
  7.2 117.0 %all-gather.3.cloned.1.call-start = ((), (), s32[]{:S(2)}) async-start(), calls=%async_computation | async-start | bytes 17825792 | tf_op jit(solution)/shard_map/all_gather | solution.py:114
  8.6 0.5 copy-start.21
  9.1 4.5 copy-start.2
  13.6 2.3 copy-start.26
  13.6 3.4 copy-start.28
  13.6 18.4 %copy-start.25 = (s32[2]{0:T(128)S(1)}, s32[2]{0:T(128)}, u32[]{:S(2)}) copy-start(s32[2]{0:T(128)} %constant.168.clone) | copy-start | bytes 28
  14.7 29.0 %collective-permute-start = (bf16[2,18,128,128]{3,2,1,0:T(8,128)(2,1)}, bf16[2,18,128,128]{3,2,1,0:T(8,128)(2,1)S(1)}, u32[]{:S(2)}, u32[]{:S(2)}) collective-permute-start(bf16[2,18,128,128]{3,2,1,0:T(8,128)(2,1)} %get-tuple-element.585), channel_id=1, source_target_pairs={{0,32},{32,64},{64,96},{1,33},{33,65},{65,97},{2,34},{34,66},{66,9... | collective-permute-start | bytes 3538952 | tf_op jit(solution)/shard_map/ppermute | solution.py:14
  16.0 16.0 %collective-permute-start.3 = (s32[2]{0:T(128)S(1)}, s32[2]{0:T(128)S(1)}, u32[]{:S(2)}, u32[]{:S(2)}) collective-permute-start(s32[2]{0:T(128)S(1)} %bitcast.620), channel_id=1, source_target_pairs={{0,1},{1,0},{2,3},{3,2},{4,5},{5,4},{6,7},{7,6},{8,9},{9,8},{10,11... | collective-permute-start | bytes 32 | tf_op jit(solution)/shard_map/ppermute | solution.py:18
  43.7 1.8 copy-start.8
  45.6 105.5 %collective-permute-start.1 = (bf16[2,18,128,128]{3,2,1,0:T(8,128)(2,1)S(1)}, bf16[2,18,128,128]{3,2,1,0:T(8,128)(2,1)}, u32[]{:S(2)}, u32[]{:S(2)}) collective-permute-start(bf16[2,18,128,128]{3,2,1,0:T(8,128)(2,1)S(1)} %get-tuple-element.587), channel_id=1, source_target_pairs={{0,32},{32,64},{64,96},{1,33},{33,65},{65,97},{2,34},{34,66},{66,9... | collective-permute-start | bytes 3538952 | tf_op jit(solution)/shard_map/ppermute | solution.py:14
  150.3 102.8 %collective-permute-start.4 = (bf16[2,2,128,2048]{3,1,2,0:T(2,128)(2,1)}, bf16[2,2,128,2048]{3,1,2,0:T(2,128)(2,1)}, u32[]{:S(2)}, u32[]{:S(2)}) collective-permute-start(bf16[2,2,128,2048]{3,1,2,0:T(2,128)(2,1)} %fusion.233), channel_id=1, source_target_pairs={{0,1},{1,0},{2,3},{3,2},{4,5},{5,4},{6,7},{7,6},{8,9},{9,8},{10,11... | collective-permute-start | bytes 6291464 | tf_op jit(solution)/shard_map/ppermute | solution.py:18
  151.2 11.4 %copy-start = (bf16[1,2,128,2048]{3,2,1,0:T(8,128)(2,1)S(1)}, bf16[1,2,128,2048]{3,2,1,0:T(8,128)(2,1)}, u32[]{:S(2)}) copy-start(bf16[1,2,128,2048]{3,2,1,0:T(8,128)(2,1)} %param.39) | copy-start | bytes 3145732
  151.2 11.4 %copy-start.22 = (bf16[2,128]{1,0:T(2,128)(2,1)S(1)}, bf16[2,128]{1,0:T(2,128)(2,1)}, u32[]{:S(2)}) copy-start(bf16[2,128]{1,0:T(2,128)(2,1)} %copy-done.21) | copy-start | bytes 1540
  151.6 98.8 %collective-permute-start.2 = (bf16[2,18,128,128]{3,2,1,0:T(8,128)(2,1)S(1)}, bf16[2,18,128,128]{3,2,1,0:T(8,128)(2,1)}, u32[]{:S(2)}, u32[]{:S(2)}) collective-permute-start(bf16[2,18,128,128]{3,2,1,0:T(8,128)(2,1)S(1)} %get-tuple-element.589), channel_id=1, source_target_pairs={{0,32},{32,64},{64,96},{1,33},{33,65},{65,97},{2,34},{34,66},{66,9... | collective-permute-start | bytes 3538952 | tf_op jit(solution)/shard_map/ppermute | solution.py:14
  162.5 87.9 %copy-start.9 = (bf16[2,18,128,128]{3,2,1,0:T(8,128)(2,1)S(1)}, bf16[2,18,128,128]{3,2,1,0:T(8,128)(2,1)}, u32[]{:S(2)}) copy-start(bf16[2,18,128,128]{3,2,1,0:T(8,128)(2,1)} %copy-done.8) | copy-start | bytes 3538948
  265.8 3.9 copy-start.27
  269.7 199.8 %copy-start.23 = (f32[2,128]{1,0:T(2,128)S(1)}, f32[2,128]{1,0:T(2,128)}, u32[]{:S(2)}) copy-start(f32[2,128]{1,0:T(2,128)} %get-tuple-element.729) | copy-start | bytes 3076
  269.7 199.8 %copy-start.24 = (f32[1,2]{1,0:T(1,128)S(1)}, f32[1,2]{1,0:T(1,128)}, u32[]{:S(2)}) copy-start(f32[1,2]{1,0:T(1,128)} %param.45) | copy-start | bytes 28
  269.7 5.2 copy-start.4
  368.0 1.6 copy-start.5
  369.6 5.1 copy-start.4
  467.8 1.6 copy-start.5
  469.5 55.0 %copy-start.1 = (bf16[1,2,128,2048]{3,2,1,0:T(8,128)(2,1)S(1)}, bf16[1,2,128,2048]{3,2,1,0:T(8,128)(2,1)}, u32[]{:S(2)}) copy-start(bf16[1,2,128,2048]{3,2,1,0:T(8,128)(2,1)} %param.39) | copy-start | bytes 3145732
  469.5 55.0 %copy-start.3 = (bf16[2,18,128,128]{3,2,1,0:T(8,128)(2,1)S(1)}, bf16[2,18,128,128]{3,2,1,0:T(8,128)(2,1)}, u32[]{:S(2)}) copy-start(bf16[2,18,128,128]{3,2,1,0:T(8,128)(2,1)} %get-tuple-element.728) | copy-start | bytes 3538948
  531.7 1.7 copy-start.20
  533.4 7.2 %copy-start.14 = (bf16[2,4,128,128]{2,3,1,0:T(8,128)(2,1)S(1)}, bf16[2,4,128,128]{2,3,1,0:T(8,128)(2,1)}, u32[]{:S(2)}) copy-start(bf16[2,4,128,128]{2,3,1,0:T(8,128)(2,1)} %get-tuple-element.1133) | copy-start | bytes 786436 | tf_op jit(solution)/shard_map/cond/branch_1_fun/while
  542.4 1.7 copy-start.20
  544.2 7.2 %copy-start.14 = (bf16[2,4,128,128]{2,3,1,0:T(8,128)(2,1)S(1)}, bf16[2,4,128,128]{2,3,1,0:T(8,128)(2,1)}, u32[]{:S(2)}) copy-start(bf16[2,4,128,128]{2,3,1,0:T(8,128)(2,1)} %get-tuple-element.1133) | copy-start | bytes 786436 | tf_op jit(solution)/shard_map/cond/branch_1_fun/while
  555.1 7.2 %copy-start.11 = (bf16[2,4,128,128]{2,3,1,0:T(8,128)(2,1)S(1)}, bf16[2,4,128,128]{2,3,1,0:T(8,128)(2,1)}, u32[]{:S(2)}) copy-start(bf16[2,4,128,128]{2,3,1,0:T(8,128)(2,1)} %get-tuple-element.1151) | copy-start | bytes 786436 | tf_op jit(solution)/shard_map/cond/branch_1_fun/while
  565.8 7.2 %copy-start.11 = (bf16[2,4,128,128]{2,3,1,0:T(8,128)(2,1)S(1)}, bf16[2,4,128,128]{2,3,1,0:T(8,128)(2,1)}, u32[]{:S(2)}) copy-start(bf16[2,4,128,128]{2,3,1,0:T(8,128)(2,1)} %get-tuple-element.1151) | copy-start | bytes 786436 | tf_op jit(solution)/shard_map/cond/branch_1_fun/while
Sparse Core Ops, SparseCore 0:
  11.7 112.4 all-gather.2
